TPU v7x, 128 devices: a whole 4x4x4 slice. The times are simulated.
128 devices in a mesh: ctx: 32 (over y, x, core), tp: 4 (over z).
Axes of the slice: x: 4, y: 4, z: 4, core: 2. Of those that a mesh axis runs over, the one named last changes fastest.
Arguments:
- hidden: bfloat16 [8192, 5120], P('ctx', 'tp'), may hold values from -6 to 6
- queries: bfloat16 [8192, 5120], P('ctx', 'tp'), may hold values from -28 to 28
- key_weight: bfloat16 [5120, 1024], P(None, 'tp'), may hold values from -0.078125 to 0.078125
- value_weight: bfloat16 [5120, 1024], P(None, 'tp'), may hold values from -0.078125 to 0.078125
- parents: int32 [64], replicated, may hold values from -1 to 62, as said below
- upstream: bfloat16 [8192, 5120], P('ctx', 'tp'), may hold values from -6 to 6
Outputs:
- attention: bfloat16 [8192, 5120], P('ctx', 'tp')
- query_grad: bfloat16 [8192, 5120], P('ctx', 'tp')
- hidden_grad: bfloat16 [8192, 5120], P('ctx', 'tp')
- key_weight_grad: float32 [5120, 1024], P('ctx', 'tp')
- value_weight_grad: float32 [5120, 1024], P('ctx', 'tp')
Inputs may be any that keep to these rules, and one draw needn't show every extreme that they name: Node blocks lie in depth-first order: parents[b] < b is the parent of block b for b > 0, parents[0] = -1 and block 0 is the only root; no root-to-leaf path holds more than 8 blocks; the last 7 blocks form one chain below block 0, so that the last block's path holds exactly 8 blocks.
All inputs are finite; a program needn't handle non-finite values.
Results may differ from a plain program's by a relative error of at most 0.023.
The roundings to bfloat16 on the way count: a program that leaves them out, or rounds other values in their place, can miss the bound.
Values may be sent and summed in bfloat16 or wider, within the bound.
No kernel may reach another device: no remote copies, remote signals or barrier semaphores. Data moves between devices by JAX's collectives and lax.ppermute only.
A program may use at most 128 MiB of HBM per device.

v0:
```python
from functools import partial
import math
import jax
import jax.numpy as jnp
from jax import lax
from jax.sharding import PartitionSpec as P

HD = 128
BLOCK = 128
DEPTH = 8
THETA = 1000000.0
NEGATIVE = -1e30
HIGHEST = lax.Precision.HIGHEST


def tree_tables(parents, block_total, depth_slots):
    indices = jnp.arange(block_total, dtype=jnp.int32)
    parent_link = (parents[:, None] == indices[None, :]).astype(jnp.float32)
    closure = jnp.eye(block_total, dtype=jnp.float32) + parent_link
    for repeat in range(depth_slots.bit_length()):
        closure = jnp.minimum(
            jnp.dot(closure, closure, precision=HIGHEST, preferred_element_type=jnp.float32), 1.0
        )
    closure_int = closure.astype(jnp.int32)
    depths = jnp.sum(closure_int, axis=1) - 1
    levels = jnp.arange(depth_slots, dtype=jnp.int32)
    select = closure_int[:, :, None] * (depths[None, :, None] == levels[None, None, :]).astype(
        jnp.int32
    )
    path_ids = jnp.sum(select * indices[None, :, None], axis=1) + jnp.sum(select, axis=1) - 1
    return (depths, path_ids)


def rope_angles(depths, block_len, head_width):
    offset = jnp.arange(block_len, dtype=jnp.int32)
    position = (depths[:, None] * block_len + offset[None, :]).astype(jnp.float32)
    midpoint = head_width // 2
    frequency = jnp.exp(
        jnp.arange(midpoint, dtype=jnp.float32) * (-2.0 * math.log(THETA) / head_width)
    )
    angles = position[:, :, None] * frequency[None, None, :]
    return (jnp.cos(angles), jnp.sin(angles))


def rotate_pairs(fields, cosine, sine_table, direction):
    midpoint = fields.shape[-1] // 2
    leading = fields[..., :midpoint]
    trailing = fields[..., midpoint:]
    cos_part = cosine[:, :, None, :]
    sin_part = direction * sine_table[:, :, None, :]
    return jnp.concatenate(
        [leading * cos_part - trailing * sin_part, trailing * cos_part + leading * sin_part],
        axis=-1,
    )


def allowed_mask(depths, block_len, slot_count):
    query_pos = jnp.arange(block_len, dtype=jnp.int32)
    key_index = jnp.arange(slot_count * block_len, dtype=jnp.int32)
    key_slot = key_index // block_len
    key_offset = key_index % block_len
    earlier = key_slot[None, None, :] < depths[:, None, None]
    itself = (key_slot[None, None, :] == depths[:, None, None]) & (
        key_offset[None, None, :] <= query_pos[None, :, None]
    )
    return earlier | itself


def attend_block(query_blocks, key_rows, value_rows, allowed, upstream_blocks, score_scale):
    scores = (
        jnp.einsum("bqhgd,bkhd->bhgqk", query_blocks, key_rows, preferred_element_type=jnp.float32)
        * score_scale
    )
    scores = jnp.where(allowed[:, None, None], scores, NEGATIVE)
    maximum = jnp.max(scores, axis=-1, keepdims=True)
    weights = jnp.exp(scores - maximum)
    totals = jnp.sum(weights, axis=-1, keepdims=True)
    mixed_rows = jnp.einsum(
        "bhgqk,bkhd->bqhgd",
        weights.astype(jnp.bfloat16),
        value_rows,
        preferred_element_type=jnp.float32,
    )
    totals_rows = jnp.transpose(totals, (0, 3, 1, 2, 4))
    output = (mixed_rows / totals_rows).astype(jnp.bfloat16)
    logsum = maximum + jnp.log(totals)
    deltas = jnp.sum(upstream_blocks.astype(jnp.float32) * output.astype(jnp.float32), axis=-1)
    deltas = jnp.transpose(deltas, (0, 2, 3, 1))[..., None]
    probabilities = jnp.exp(scores - logsum)
    value_grad = jnp.einsum(
        "bhgqk,bqhgd->bkhd",
        probabilities.astype(jnp.bfloat16),
        upstream_blocks,
        preferred_element_type=jnp.float32,
    )
    prob_grad = jnp.einsum(
        "bqhgd,bkhd->bhgqk", upstream_blocks, value_rows, preferred_element_type=jnp.float32
    )
    score_grad = (probabilities * (prob_grad - deltas)).astype(jnp.bfloat16)
    query_grad = (
        jnp.einsum("bhgqk,bkhd->bqhgd", score_grad, key_rows, preferred_element_type=jnp.float32)
        * score_scale
    ).astype(jnp.bfloat16)
    key_grad = (
        jnp.einsum(
            "bhgqk,bqhgd->bkhd", score_grad, query_blocks, preferred_element_type=jnp.float32
        )
        * score_scale
    )
    return (output, query_grad, key_grad, value_grad)


def shards(hidden, queries, key_weight, value_weight, parents, upstream):
    local_rows = hidden.shape[0]
    blocks = local_rows // BLOCK
    block_total = parents.shape[0]
    key_width = key_weight.shape[1]
    key_heads = key_width // HD
    groups = queries.shape[1] // key_width
    pair_width = 2 * key_width
    score_scale = 1.0 / math.sqrt(HD)
    first_block = lax.axis_index("ctx") * blocks
    depth_all, path_all = tree_tables(parents, block_total, DEPTH)
    depths = lax.dynamic_slice_in_dim(depth_all, first_block, blocks, 0)
    path_ids = lax.dynamic_slice_in_dim(path_all, first_block, blocks, 0)
    cosine, sine_table = rope_angles(depths, BLOCK, HD)
    features = lax.all_gather(hidden, "tp", axis=1, tiled=True)
    key_linear = jnp.dot(features, key_weight, preferred_element_type=jnp.float32).reshape(
        blocks, BLOCK, key_heads, HD
    )
    key_rotated = (
        rotate_pairs(key_linear, cosine, sine_table, 1.0)
        .astype(jnp.bfloat16)
        .reshape(local_rows, key_width)
    )
    value_rows = jnp.dot(features, value_weight, preferred_element_type=jnp.float32).astype(
        jnp.bfloat16
    )
    key_value = jnp.concatenate([key_rotated, value_rows], axis=1)
    gathered = lax.all_gather(key_value, "ctx", axis=0, tiled=True).reshape(
        block_total, BLOCK, pair_width
    )
    slot_rows = gathered[jnp.clip(path_ids, 0, block_total - 1)]
    query_blocks = queries.reshape(blocks, BLOCK, key_heads, groups, HD)
    upstream_blocks = upstream.reshape(blocks, BLOCK, key_heads, groups, HD)

    def attend_slots(slot_count):
        chosen = slot_rows[:, :slot_count].reshape(blocks, slot_count * BLOCK, pair_width)
        key_part = chosen[..., :key_width].reshape(blocks, slot_count * BLOCK, key_heads, HD)
        value_part = chosen[..., key_width:].reshape(blocks, slot_count * BLOCK, key_heads, HD)
        allowed = allowed_mask(depths, BLOCK, slot_count)
        output, query_grad, key_grad, value_grad = attend_block(
            query_blocks, key_part, value_part, allowed, upstream_blocks, score_scale
        )
        slot_grads = jnp.concatenate(
            [
                key_grad.reshape(blocks, slot_count, BLOCK, key_width),
                value_grad.reshape(blocks, slot_count, BLOCK, key_width),
            ],
            axis=-1,
        )
        slot_grads = jnp.pad(slot_grads, ((0, 0), (0, DEPTH - slot_count), (0, 0), (0, 0)))
        return (
            output.reshape(local_rows, groups * key_width),
            query_grad.reshape(local_rows, groups * key_width),
            slot_grads,
        )

    needed = jnp.max(depths) + 1
    bucket = (needed > DEPTH // 4).astype(jnp.int32) + (needed > DEPTH // 2).astype(jnp.int32)
    bucket_sizes = [DEPTH // 4, DEPTH // 2, DEPTH]
    attention, query_grad, slot_grads = lax.switch(
        bucket, [partial(attend_slots, slot_count) for slot_count in bucket_sizes]
    )
    flat_grads = slot_grads.reshape(blocks * DEPTH, BLOCK * pair_width)
    block_targets = path_ids.reshape(blocks * DEPTH)
    block_count = local_rows * lax.axis_size("ctx") // BLOCK
    selector = (block_targets[None, :] == jnp.arange(block_count, dtype=jnp.int32)[:, None]).astype(
        jnp.float32
    )
    pair_grads = lax.psum_scatter(
        jnp.dot(
            selector, flat_grads, precision=HIGHEST, preferred_element_type=jnp.float32
        ).reshape(local_rows * lax.axis_size("ctx"), pair_width),
        "ctx",
        scatter_dimension=0,
        tiled=True,
    )
    key_total = pair_grads[:, :key_width].reshape(blocks, BLOCK, key_heads, HD)
    key_linear_grad = (
        rotate_pairs(key_total, cosine, sine_table, -1.0)
        .astype(jnp.bfloat16)
        .reshape(local_rows, key_width)
    )
    value_grad_rows = pair_grads[:, key_width:].astype(jnp.bfloat16)
    grad_pairs = jnp.concatenate([key_linear_grad, value_grad_rows], axis=1)
    weight_grads = lax.psum_scatter(
        jnp.einsum("tc,tw->cw", features, grad_pairs, preferred_element_type=jnp.float32),
        "ctx",
        scatter_dimension=0,
        tiled=True,
    )
    partial_input = jnp.einsum(
        "tw,dw->td", key_linear_grad, key_weight, preferred_element_type=jnp.float32
    )
    partial_input = partial_input + jnp.einsum(
        "tw,dw->td", value_grad_rows, value_weight, preferred_element_type=jnp.float32
    )
    hidden_grad = lax.psum_scatter(
        partial_input.astype(jnp.bfloat16), "tp", scatter_dimension=1, tiled=True
    )
    return (
        attention,
        query_grad,
        hidden_grad,
        weight_grads[:, :key_width],
        weight_grads[:, key_width:],
    )


def solution(mesh):
    return jax.shard_map(
        shards,
        mesh=mesh,
        in_specs=(
            P("ctx", "tp"),
            P("ctx", "tp"),
            P(None, "tp"),
            P(None, "tp"),
            P(),
            P("ctx", "tp"),
        ),
        out_specs=(P("ctx", "tp"), P("ctx", "tp"), P("ctx", "tp"), P("ctx", "tp"), P("ctx", "tp")),
        check_vma=False,
    )
```

profile of v0, /device:TPU:1, one launch (start us, length us, event | category | flops | bytes accessed | tf_op | source)
XLA Modules:
  0.0 535.3 jit_solution(10421093804757671469)
XLA Ops:
  7.2 0.7 all-gather.3.cloned.1.call-update
  8.0 1.0 convolution_minimum_fusion.3
  9.0 0.2 convolution_minimum_fusion.2
  9.1 0.2 convolution_minimum_fusion.1
  9.3 0.9 fusion.127
  10.3 1.3 broadcast_multiply_fusion
  11.6 36.5 %all-gather.3.cloned.1.call-done = bf16[256,5120]{1,0:T(8,128)(2,1)} async-done(((bf16[256,1280]{1,0:T(8,128)(2,1)}), bf16[256,5120]{1,0:T(8,128)(2,1)}) %all-gather.3.cloned.1.call-update) | async-done | bytes 2621456 | tf_op jit(solution)/shard_map/all_gather | solution.py:127
  48.1 2.6 fusion.129
  50.7 0.1 reshape.522
  50.8 1.5 subtract_convert_fusion.1
  52.4 0.4 pad_maximum_fusion.2
  52.9 3.7 convolution_convert_fusion
  56.5 0.7 pad_maximum_fusion.1
  57.3 0.6 reduce_max.36
  58.6 3.0 fusion.108
  61.6 0.7 eq.104
  62.3 54.3 %all-gather.5.cloned.1.call-done = bf16[8192,512]{0,1:T(8,128)(2,1)} async-done(((bf16[256,512]{0,1:T(8,128)(2,1)}), bf16[8192,512]{0,1:T(8,128)(2,1)}) %all-gather.5.cloned.1.call-update) | async-done | bytes 8388624 | tf_op jit(solution)/shard_map/all_gather | solution.py:140
  116.6 96.7 %conditional.1 = (f32[16,65536]{1,0:T(8,128)}, bf16[256,1280]{1,0:T(8,128)(2,1)}, bf16[256,1280]{1,0:T(8,128)(2,1)}) conditional(s32[]{:T(128)} %clamp.4, (s32[2]{0:T(128)S(1)}, bf16[8192,512]{0,1:T(8,128)(2,1)}, s32[]{:T(128)}, bf16[256,1280]{1,0:T(8,128)(2,1)S(1)}, bf16[256,1280]{1,0:T(8,128)(2,1)}, ...), branch_computations={%region_4.8_spmd.clone, %region_8.12_spmd.clone, %region_12.16_spm... | conditional | flops 4086446080 | bytes 220787328 | solution.py:172
  123.4 0.1 iota_compare_fusion.3
  123.5 0.3 and_or_fusion.1
  123.9 1.7 reshape.603
  125.6 2.6 reshape.617
  128.1 2.4 copy.374
  130.5 12.0 %copy.377 = bf16[8192,512]{1,0:T(8,128)(2,1)} copy(bf16[8192,512]{0,1:T(8,128)(2,1)} %get-tuple-element.247) | data formatting | bytes 16777216 | tf_op jit(solution)/shard_map
  142.5 5.4 %gather_fusion.1 = bf16[16,128,512]{2,1,0:T(8,128)(2,1)} fusion(bf16[64,128,512]{2,1,0:T(8,128)(2,1)} %bitcast.314, s32[1024]{0:T(1024)S(1)} %pad_clamp_fusion.1), kind=kCustom, calls=%fused_computation.1.clone | custom fusion | bytes 4194368 | tf_op jit(solution)/shard_map/gather | solution.py:143
  147.9 1.3 slice.74
  149.2 0.9 fusion.124
  150.1 1.0 copy.397
  151.1 1.3 copy.396
  152.4 2.4 fusion.30
  154.8 1.1 fusion.26
  155.9 0.4 copy-done.19
  156.3 0.6 copy-done.21
  156.9 2.4 multiply_reduce_fusion.1
  159.3 2.6 copy.380
  161.9 2.7 reshape.604
  164.7 5.0 fusion.46
  169.7 4.3 fusion.25
  174.0 0.9 fusion.51
  174.9 1.9 fusion.52
  176.8 1.8 copy.375
  178.6 3.1 reshape.599
  181.7 3.1 copy.376
  184.8 3.1 reshape.600
  187.9 1.5 copy.381
  189.4 2.6 reshape.605
  191.9 2.1 fusion.29
  194.0 4.5 copy.407
  213.3 12.3 %fusion.115 = f32[64,65536]{1,0:T(8,128)} fusion(f32[16,65536]{1,0:T(8,128)} %get-tuple-element.101, s32[16]{0:T(128)} %eq.104), kind=kOutput, calls=%fused_computation.186 | convolution fusion | flops 805307392 | bytes 20971584 | tf_op jit(solution)/shard_map/dot_general | solution.py:182
  225.5 14.5 %reshape.523 = f32[8192,512]{1,0:T(8,128)} reshape(f32[64,65536]{1,0:T(8,128)} %fusion.115) | data formatting | bytes 33554432 | tf_op jit(solution)/shard_map/reshape | solution.py:184
  240.1 131.5 %reduce-scatter.6.cloned.1.call-done = f32[256,512]{1,0:T(8,128)} async-done(((f32[8192,512]{1,0:T(8,128)}), f32[256,512]{1,0:T(8,128)}) %reduce-scatter.6.cloned.1.call-update) | async-done | bytes 524304 | tf_op jit(solution)/shard_map/reduce_scatter | solution.py:181
  371.6 1.0 slice.81
  372.6 0.1 reshape.524
  372.8 0.5 subtract_convert_fusion
  373.3 0.4 pad_maximum_fusion.3
  373.7 1.0 slice.96
  374.6 7.1 %convolution_bitcast_fusion.3 = f32[5120,512]{0,1:T(8,128)} fusion(bf16[256,5120]{1,0:T(8,128)(2,1)} %all-gather.3.cloned.1.call-done, bf16[256,256]{1,0:T(8,128)(2,1)S(1)} %slice.96, bf16[256,256]{1,0:T(8,128)(2,1)S(1)} %bitcast.337), kind=kOutput, calls=%fused_computation.152 | convolution fusion | flops 1342701568 | bytes 13369344 | tf_op jit(solution)/shard_map/tc,tw->cw/dot_general | solution.py:198
  381.8 11.4 %copy.336 = f32[5120,512]{1,0:T(8,128)} copy(f32[5120,512]{0,1:T(8,128)} %convolution_bitcast_fusion.3) | data formatting | bytes 20971520
  393.2 0.9 fusion.121
  394.2 0.9 copy-done.5
  395.1 2.5 fusion.106
  397.6 92.8 %reduce-scatter.10.cloned.1.call-done = f32[160,512]{1,0:T(8,128)} async-done(((f32[5120,512]{1,0:T(8,128)}), f32[160,512]{1,0:T(8,128)}) %reduce-scatter.10.cloned.1.call-update) | async-done | bytes 327696
  490.4 1.7 fusion.126
  492.1 36.4 %reduce-scatter.8.cloned.1.call-done = bf16[256,1280]{1,0:T(8,128)(2,1)} async-done(((bf16[256,5120]{1,0:T(8,128)(2,1)}), bf16[256,1280]{1,0:T(8,128)(2,1)}) %reduce-scatter.8.cloned.1.call-update) | async-done | bytes 655376 | tf_op jit(solution)/shard_map/reduce_scatter | solution.py:209
  (48 shorter events, 0.9 us)
Async XLA Ops:
  7.2 40.9 %copy-start = (bf16[5120,256]{1,0:T(8,128)(2,1)S(1)}, bf16[5120,256]{1,0:T(8,128)(2,1)}, u32[]{:S(2)}) copy-start(bf16[5120,256]{1,0:T(8,128)(2,1)} %param.11) | copy-start | bytes 7864324
  7.2 40.9 %all-gather.3.cloned.1.call-start = ((), (), s32[]{:S(2)}) async-start(), calls=%async_computation.3 | async-start | bytes 3276800 | tf_op jit(solution)/shard_map/all_gather | solution.py:127
  7.9 108.7 %all-gather.5.cloned.1.call-start = ((), (), s32[]{:S(2)}) async-start(), calls=%async_computation.4 | async-start | bytes 8650752 | tf_op jit(solution)/shard_map/all_gather | solution.py:140
  50.8 65.8 %copy-start.8 = (bf16[256,1280]{1,0:T(8,128)(2,1)S(1)}, bf16[256,1280]{1,0:T(8,128)(2,1)}, u32[]{:S(2)}) copy-start(bf16[256,1280]{1,0:T(8,128)(2,1)} %param.10) | copy-start | bytes 1966084
  57.3 314.4 %reduce-scatter.6.cloned.1.call-start = ((), (), s32[]{:S(2)}) async-start(), calls=%async_computation.5 | async-start | bytes 17301504 | tf_op jit(solution)/shard_map/reduce_scatter | solution.py:181
  154.8 4.6 copy-start.4
  154.8 1.6 copy-start.19
  154.8 2.1 copy-start.21
  164.7 5.0 copy-start.20
  164.7 5.0 copy-start.22
  169.7 4.3 copy-start.11
  176.8 11.1 %copy-start.12 = (bf16[2,128,2,5,128]{4,1,3,2,0:T(8,128)(2,1)S(1)}, bf16[2,128,2,5,128]{4,1,3,2,0:T(8,128)(2,1)}, u32[]{:S(2)}) copy-start(bf16[2,128,2,5,128]{4,1,3,2,0:T(8,128)(2,1)} %fusion.52) | copy-start | bytes 1966084 | tf_op jit(solution)/shard_map/cond
  240.1 132.7 %copy-start.14 = (f32[2,128,64]{2,1,0:T(8,128)S(1)}, f32[2,128,64]{2,1,0:T(8,128)}, u32[]{:S(2)}) copy-start(f32[2,128,64]{2,1,0:T(8,128)} %get-tuple-element.306) | copy-start | bytes 196612
  240.1 132.7 %copy-start.23 = (f32[2,128,64]{2,1,0:T(8,128)S(1)}, f32[2,128,64]{2,1,0:T(8,128)}, u32[]{:S(2)}) copy-start(f32[2,128,64]{2,1,0:T(8,128)} %get-tuple-element.304) | copy-start | bytes 196612
  240.1 250.3 %reduce-scatter.10.cloned.1.call-start = ((), (), s32[]{:S(2)}) async-start(), calls=%async_computation.7 | async-start | bytes 10813440
  393.2 1.0 copy-start.18
  393.2 135.4 %reduce-scatter.8.cloned.1.call-start = ((), (), s32[]{:S(2)}) async-start(), calls=%async_computation.6 | async-start | bytes 3276800 | tf_op jit(solution)/shard_map/reduce_scatter | solution.py:209
  393.2 1.9 copy-start.5
Sparse Core Ops, SparseCore 0:
  9.6 38.4 all-gather.2
  57.4 59.1 all-gather.4
  240.2 131.3 reduce-scatter.5
  393.3 97.0 reduce-scatter.9
  493.2 35.3 reduce-scatter.7
where the time goes:
time: 541 us; the launch traced here: 535 us
  waiting for transfers between devices  352 us (65%)
  local copies, waits for them, and re-layouts  86.2 us (16%)
  matrix products  48 us (9%)
  loops' own time  21.5 us (4%)
  between operations  14.9 us (3%)
  other arithmetic  12.3 us (2%)
    reduce_scatter x1, waiting for transfers between devices, shards(): lax.psum_scatter(jnp.dot(selector, flat_grads, precision=HIGHEST, preferr...  132 us
    unnamed x6, waiting for transfers between devices  93.5 us
    all_gather x1, waiting for transfers between devices, shards(): lax.all_gather(key_value, 'ctx', axis=0, tiled=True)  54.3 us
    all_gather x1, waiting for transfers between devices, shards(): features = lax.all_gather(hidden, 'tp', axis=1, tiled=True)  36.5 us
    reduce_scatter x1, waiting for transfers between devices, shards(): lax.psum_scatter(partial_input.astype(jnp.bfloat16), 'tp', scatter_dimens...  36.4 us
    another operation x1, loops' own time, shards(): lax.switch(bucket, [partial(attend_slots, slot_count) for slot_count in b...  21.5 us
    cond x21, local copies, waits for them, and re-layouts  17.2 us
    reshape x1, local copies, waits for them, and re-layouts, shards(): pair_grads = lax.psum_scatter(jnp.dot(selector, flat_grads, precision=HIG...  14.5 us
  transfers between devices with their start and end apart: 5, of which 5 were waited for; matrix products, arithmetic and copies ran while one was open for 2% of the time, Pallas kernels for 0%

commit v1 on v0

--- a/solution.py
+++ b/solution.py
@@ -11,6 +11,11 @@
 THETA = 1000000.0
 NEGATIVE = -1e30
 HIGHEST = lax.Precision.HIGHEST
+
+
+def swapped_in(x, name, along):
+    sent = jnp.stack([x] * lax.axis_size(name))
+    return jnp.concatenate(lax.all_to_all(sent, name, 0, 0), axis=along)
 
 
 def tree_tables(parents, block_total, depth_slots):
@@ -137,9 +142,7 @@
         jnp.bfloat16
     )
     key_value = jnp.concatenate([key_rotated, value_rows], axis=1)
-    gathered = lax.all_gather(key_value, "ctx", axis=0, tiled=True).reshape(
-        block_total, BLOCK, pair_width
-    )
+    gathered = swapped_in(key_value, "ctx", 0).reshape(block_total, BLOCK, pair_width)
     slot_rows = gathered[jnp.clip(path_ids, 0, block_total - 1)]
     query_blocks = queries.reshape(blocks, BLOCK, key_heads, groups, HD)
     upstream_blocks = upstream.reshape(blocks, BLOCK, key_heads, groups, HD)

time: 541 us -> 582 us (1.076)
  waiting for transfers between devices: 352 us -> 397 us
  starting transfers between devices: 0.2 us -> 8.04 us
  local copies, waits for them, and re-layouts: 86.2 us -> 79.2 us
    all_to_all x0 -> x1, waiting for transfers between devices: none -> 96.5 us  [swapped_in(): return jnp.concatenate(lax.all_to_all(sent, name, 0, 0), axis=along)]
    all_gather x1 -> x0, waiting for transfers between devices: 54.3 us -> none  [shards(): lax.all_gather(key_value, 'ctx', axis=0, tiled=True)]
    all_to_all x0 -> x1, starting transfers between devices: none -> 7.88 us  [swapped_in(): return jnp.concatenate(lax.all_to_all(sent, name, 0, 0), axis=along)]
    another operation x1, local copies, waits for them, and re-layouts: 12 us -> 4.16 us  [swapped_in(): sent = jnp.stack([x] * lax.axis_size(name))]
    cond x21 -> x17, local copies, waits for them, and re-layouts: 17.2 us -> 18.4 us
    unnamed x6 -> x5, waiting for transfers between devices: 93.5 us -> 93.4 us
    unnamed x15 -> x17, local copies, waits for them, and re-layouts: 12.4 us -> 12.4 us
where the time goes in v1:
time: 582 us; the launch traced here: 576 us
  waiting for transfers between devices  397 us (68%)
  local copies, waits for them, and re-layouts  79.2 us (14%)
  matrix products  46.5 us (8%)
  loops' own time  21.3 us (4%)
  between operations  14.9 us (3%)
  other arithmetic  9.71 us (2%)
  starting transfers between devices  8.04 us (1%)
    reduce_scatter x1, waiting for transfers between devices, shards(): lax.psum_scatter(jnp.dot(selector, flat_grads, precision=HIGHEST, preferr...  133 us
    all_to_all x1, waiting for transfers between devices, swapped_in(): return jnp.concatenate(lax.all_to_all(sent, name, 0, 0), axis=along)  96.5 us
    unnamed x5, waiting for transfers between devices  93.4 us
    all_gather x1, waiting for transfers between devices, shards(): features = lax.all_gather(hidden, 'tp', axis=1, tiled=True)  37.2 us
    reduce_scatter x1, waiting for transfers between devices, shards(): lax.psum_scatter(partial_input.astype(jnp.bfloat16), 'tp', scatter_dimens...  36.5 us
    another operation x1, loops' own time, shards(): lax.switch(bucket, [partial(attend_slots, slot_count) for slot_count in b...  21.3 us
    cond x17, local copies, waits for them, and re-layouts  18.4 us
    reshape x1, local copies, waits for them, and re-layouts, shards(): pair_grads = lax.psum_scatter(jnp.dot(selector, flat_grads, precision=HIG...  14.5 us
  transfers between devices with their start and end apart: 5, of which 5 were waited for; matrix products, arithmetic and copies ran while one was open for 2% of the time, Pallas kernels for 0%

profile of v1, /device:TPU:1, one launch (start us, length us, event | category | flops | bytes accessed | tf_op | source)
XLA Modules:
  0.0 576.2 jit_solution(13633197445151742542)
XLA Ops:
  7.2 0.7 all-gather.2.cloned.1.call-update
  7.9 1.0 convolution_minimum_fusion.3
  8.9 0.2 convolution_minimum_fusion.2
  9.1 0.2 convolution_minimum_fusion.1
  9.2 0.3 fusion.127
  9.7 1.2 broadcast_multiply_fusion
  10.9 37.2 %all-gather.2.cloned.1.call-done = bf16[256,5120]{1,0:T(8,128)(2,1)} async-done(((bf16[256,1280]{1,0:T(8,128)(2,1)}), bf16[256,5120]{1,0:T(8,128)(2,1)}) %all-gather.2.cloned.1.call-update) | async-done | bytes 2621456 | tf_op jit(solution)/shard_map/all_gather | solution.py:132
  48.1 2.6 fusion.129
  50.6 0.1 reshape.514
  50.8 0.5 subtract_convert_fusion.1
  51.3 0.4 pad_maximum_fusion.2
  51.8 3.7 convolution_convert_fusion
  55.5 0.1 copy.271
  55.6 4.2 stack.2
  59.8 7.9 %all-to-all-start = ((bf16[32,256,512]{2,1,0:T(8,128)(2,1)}), bf16[32,256,512]{2,1,0:T(8,128)(2,1)}, u32[]{:S(2)}, u32[]{:S(2)}) async-start(bf16[32,256,512]{2,1,0:T(8,128)(2,1)} %stack.2), calls=%async_computation | async-start | bytes 16777216 | tf_op jit(solution)/shard_map/all_to_all | solution.py:18
  67.7 0.6 reduce_max.36
  69.0 2.2 fusion.108
  71.3 0.6 eq.104
  71.9 96.5 %all-to-all-done = bf16[32,256,512]{2,1,0:T(8,128)(2,1)} async-done(((bf16[32,256,512]{2,1,0:T(8,128)(2,1)}), bf16[32,256,512]{2,1,0:T(8,128)(2,1)}, u32[]{:S(2)}, u32[]{:S(2)}) %all-to-all-start) | async-done | bytes 8388640 | tf_op jit(solution)/shard_map/all_to_all | solution.py:18
  168.4 84.3 %conditional.1 = (f32[16,65536]{1,0:T(8,128)}, bf16[256,1280]{1,0:T(8,128)(2,1)}, bf16[256,1280]{1,0:T(8,128)(2,1)}) conditional(s32[]{:T(128)} %clamp.4, (s32[2]{0:T(128)S(1)}, bf16[32,256,512]{2,1,0:T(8,128)(2,1)}, s32[]{:T(128)}, bf16[256,1280]{1,0:T(8,128)(2,1)S(1)}, bf16[256,1280]{1,0:T(8,128)(2,1)}, ...), branch_computations={%region_4.8_spmd.clone, %region_8.12_spmd.clone, %region_12.16_spm... | conditional | flops 4086446080 | bytes 204010112 | solution.py:175
  175.0 5.4 gather_fusion.1
  180.4 1.3 slice.74
  181.7 1.0 fusion.124
  182.8 2.1 copy.384
  185.0 0.3 and_or_fusion.1
  185.4 2.1 copy.383
  187.4 1.7 reshape.595
  189.1 2.5 reshape.609
  191.7 1.7 copy.363
  193.4 2.5 fusion.30
  196.0 1.1 fusion.26
  197.1 0.3 copy-done.20
  197.4 2.4 multiply_reduce_fusion.1
  199.8 2.6 copy.368
  202.4 2.7 reshape.596
  205.1 4.8 fusion.46
  209.9 4.3 fusion.25
  214.3 0.9 fusion.51
  215.1 0.2 copy-done.11
  215.3 1.1 fusion.52
  216.4 1.9 copy.364
  218.2 3.1 reshape.591
  221.3 3.0 copy.365
  224.3 3.1 reshape.592
  227.4 1.4 copy.369
  228.9 2.6 reshape.597
  231.4 2.1 fusion.29
  233.6 4.5 copy.394
  252.8 12.3 %fusion.115 = f32[64,65536]{1,0:T(8,128)} fusion(f32[16,65536]{1,0:T(8,128)} %get-tuple-element.101, s32[16]{0:T(128)} %eq.104), kind=kOutput, calls=%fused_computation.186 | convolution fusion | flops 805307392 | bytes 20971584 | tf_op jit(solution)/shard_map/dot_general | solution.py:185
  265.0 14.5 %reshape.515 = f32[8192,512]{1,0:T(8,128)} reshape(f32[64,65536]{1,0:T(8,128)} %fusion.115) | data formatting | bytes 33554432 | tf_op jit(solution)/shard_map/reshape | solution.py:187
  279.6 133.1 %reduce-scatter.6.cloned.1.call-done = f32[256,512]{1,0:T(8,128)} async-done(((f32[8192,512]{1,0:T(8,128)}), f32[256,512]{1,0:T(8,128)}) %reduce-scatter.6.cloned.1.call-update) | async-done | bytes 524304 | tf_op jit(solution)/shard_map/reduce_scatter | solution.py:184
  412.7 1.0 slice.81
  413.7 0.1 reshape.516
  413.8 0.5 subtract_convert_fusion
  414.3 0.4 pad_maximum_fusion.3
  414.7 1.0 slice.96
  415.7 7.1 %convolution_bitcast_fusion.3 = f32[5120,512]{0,1:T(8,128)} fusion(bf16[256,5120]{1,0:T(8,128)(2,1)} %all-gather.2.cloned.1.call-done, bf16[256,256]{1,0:T(8,128)(2,1)S(1)} %slice.96, bf16[256,256]{1,0:T(8,128)(2,1)S(1)} %bitcast.334), kind=kOutput, calls=%fused_computation.152 | convolution fusion | flops 1342701568 | bytes 13369344 | tf_op jit(solution)/shard_map/tc,tw->cw/dot_general | solution.py:201
  422.8 11.4 %copy.326 = f32[5120,512]{1,0:T(8,128)} copy(f32[5120,512]{0,1:T(8,128)} %convolution_bitcast_fusion.3) | data formatting | bytes 20971520
  434.3 0.9 fusion.121
  435.3 0.9 copy-done.5
  436.2 2.4 fusion.106
  438.6 92.6 %reduce-scatter.10.cloned.1.call-done = f32[160,512]{1,0:T(8,128)} async-done(((f32[5120,512]{1,0:T(8,128)}), f32[160,512]{1,0:T(8,128)}) %reduce-scatter.10.cloned.1.call-update) | async-done | bytes 327696
  531.3 1.7 fusion.126
  533.0 36.5 %reduce-scatter.8.cloned.1.call-done = bf16[256,1280]{1,0:T(8,128)(2,1)} async-done(((bf16[256,5120]{1,0:T(8,128)(2,1)}), bf16[256,1280]{1,0:T(8,128)(2,1)}) %reduce-scatter.8.cloned.1.call-update) | async-done | bytes 655376 | tf_op jit(solution)/shard_map/reduce_scatter | solution.py:212
  (46 shorter events, 1.0 us)
Async XLA Ops:
  7.2 40.9 %copy-start = (bf16[5120,256]{1,0:T(8,128)(2,1)S(1)}, bf16[5120,256]{1,0:T(8,128)(2,1)}, u32[]{:S(2)}) copy-start(bf16[5120,256]{1,0:T(8,128)(2,1)} %param.11) | copy-start | bytes 7864324
  7.2 40.9 %all-gather.2.cloned.1.call-start = ((), (), s32[]{:S(2)}) async-start(), calls=%async_computation.4 | async-start | bytes 3276800 | tf_op jit(solution)/shard_map/all_gather | solution.py:132
  10.9 44.6 %copy-start.14 = (f32[2,128,64]{2,1,0:T(8,128)}, f32[2,128,64]{2,1,0:T(8,128)S(1)}, u32[]{:S(2)}) copy-start(f32[2,128,64]{2,1,0:T(8,128)S(1)} %get-tuple-element.288) | copy-start | bytes 196612
  59.8 108.6 %copy-start.8 = (bf16[256,1280]{1,0:T(8,128)(2,1)S(1)}, bf16[256,1280]{1,0:T(8,128)(2,1)}, u32[]{:S(2)}) copy-start(bf16[256,1280]{1,0:T(8,128)(2,1)} %param.10) | copy-start | bytes 1966084
  59.8 108.6 %all-to-all-start = ((bf16[32,256,512]{2,1,0:T(8,128)(2,1)}), bf16[32,256,512]{2,1,0:T(8,128)(2,1)}, u32[]{:S(2)}, u32[]{:S(2)}) async-start(bf16[32,256,512]{2,1,0:T(8,128)(2,1)} %stack.2), calls=%async_computation | async-start | bytes 16777216 | tf_op jit(solution)/shard_map/all_to_all | solution.py:18
  67.7 345.0 %reduce-scatter.6.cloned.1.call-start = ((), (), s32[]{:S(2)}) async-start(), calls=%async_computation.5 | async-start | bytes 17301504 | tf_op jit(solution)/shard_map/reduce_scatter | solution.py:184
  195.9 3.9 copy-start.4
  196.0 1.4 copy-start.20
  205.1 4.8 copy-start.21
  209.9 4.3 copy-start.12
  214.2 1.0 copy-start.11
  279.5 134.3 %copy-start.15 = (f32[2,128,64]{2,1,0:T(8,128)S(1)}, f32[2,128,64]{2,1,0:T(8,128)}, u32[]{:S(2)}) copy-start(f32[2,128,64]{2,1,0:T(8,128)} %copy-done.14) | copy-start | bytes 196612
  279.5 134.3 %copy-start.22 = (f32[2,128,64]{2,1,0:T(8,128)S(1)}, f32[2,128,64]{2,1,0:T(8,128)}, u32[]{:S(2)}) copy-start(f32[2,128,64]{2,1,0:T(8,128)} %get-tuple-element.286) | copy-start | bytes 196612
  279.6 251.7 %reduce-scatter.10.cloned.1.call-start = ((), (), s32[]{:S(2)}) async-start(), calls=%async_computation.7 | async-start | bytes 10813440
  434.2 1.0 copy-start.19
  434.2 135.2 %reduce-scatter.8.cloned.1.call-start = ((), (), s32[]{:S(2)}) async-start(), calls=%async_computation.6 | async-start | bytes 3276800 | tf_op jit(solution)/shard_map/reduce_scatter | solution.py:212
  434.3 1.9 copy-start.5
Sparse Core Ops, SparseCore 0:
  9.6 38.3 all-gather.1
  279.7 132.9 reduce-scatter.5
  434.4 96.8 reduce-scatter.9
  534.1 35.3 reduce-scatter.7
